TPU v7x, 512 devices: a whole 4x8x8 slice. The times are simulated.
512 devices in a mesh: prow: 16 (over y, core), pcol: 32 (over z, x).
Axes of the slice: x: 4, y: 8, z: 8, core: 2. Of those that a mesh axis runs over, the one named last changes fastest.
Arguments:
- stiffness: float32 [4, 16, 2, 32, 256, 256], P(None, 'prow', None, 'pcol'), may hold values from -1 to 33, as said below
- pattern: int32 [2, 64], replicated, may hold values 0 or 1
Outputs:
- factored: float32 [4, 16, 2, 32, 256, 256], P(None, 'prow', None, 'pcol')
Inputs may be any that keep to these rules, and one draw needn't show every extreme that they name: `stiffness`: Symmetric; entries off the main diagonal have magnitude at most 1, and the main diagonal's entries lie between 31 and 33.
All inputs are finite; a program needn't handle non-finite values.
Results may differ from a plain program's by a relative error of at most 0.0003.
Values sent between devices are 32-bit elements; how exact they have to be, the bound alone decides.
A program may use at most 64 MiB of HBM per device.

v0:
```python
import jax
import jax.numpy as jnp
from jax import lax
from jax.sharding import PartitionSpec as P


def broadcast(block, axis, source):
    block = jnp.where(lax.axis_index(axis) == source, block, jnp.zeros_like(block))
    return lax.psum(block, axis)


def solve_blocks(factor, blocks):
    count = blocks.shape[0]
    order = blocks.shape[1]
    right_hand = jnp.transpose(blocks, (2, 0, 1)).reshape(order, count * order)
    solved = lax.linalg.triangular_solve(factor, right_hand, left_side=True, lower=True)
    return jnp.transpose(solved.reshape(order, count, order), (1, 2, 0))


def local(stiffness, pattern):
    row_count = stiffness.shape[0]
    col_count = stiffness.shape[2]
    order = stiffness.shape[4]
    nprow = lax.axis_size("prow")
    npcol = lax.axis_size("pcol")
    my_row = lax.axis_index("prow")
    my_col = lax.axis_index("pcol")
    blocks = stiffness.reshape(row_count, col_count, order, order)
    glob_rows = my_row + nprow * jnp.arange(row_count, dtype=jnp.int32)
    glob_cols = my_col + npcol * jnp.arange(col_count, dtype=jnp.int32)
    all_rows = jnp.arange(row_count * nprow, dtype=jnp.int32)
    first_flags = (pattern[0] == 1) & (all_rows > 0)
    second_flags = ((pattern[1] == 1) | first_flags[1] & first_flags) & (all_rows > 1)
    for column, flags in ((0, first_flags), (1, second_flags)):
        local_col = column // npcol
        local_diag = blocks[column // nprow, local_col]
        factor = broadcast(jnp.linalg.cholesky(local_diag), "prow", column % nprow)
        payload = solve_blocks(factor, blocks[:, local_col])
        row_pieces = broadcast(payload, "pcol", column % npcol)
        my_flags = jnp.take(flags, glob_rows)
        panel_blocks = jnp.where(my_flags[:, None, None], row_pieces, jnp.zeros_like(row_pieces))
        source_rows = glob_cols // nprow
        column_pieces = broadcast(
            jnp.take(panel_blocks, source_rows, axis=0), "prow", my_col % nprow
        )
        update = jnp.einsum(
            "iab,jcb->ijac", panel_blocks, column_pieces, precision=lax.Precision.HIGHEST
        )
        keep_mask = (glob_cols[None, :] > column) & (glob_cols[None, :] <= glob_rows[:, None])
        blocks = blocks - jnp.where(keep_mask[:, :, None, None], update, jnp.zeros_like(update))
        old_column = blocks[:, local_col]
        new_column = jnp.where((glob_rows > column)[:, None, None], panel_blocks, old_column)
        new_column = jnp.where((glob_rows == column)[:, None, None], factor[None, :, :], new_column)
        is_panel_col = my_col == column % npcol
        blocks = blocks.at[:, local_col].set(jnp.where(is_panel_col, new_column, old_column))
    return blocks.reshape(stiffness.shape)


def solution(mesh):
    placed = (P(None, "prow", None, "pcol", None, None), P())
    return jax.shard_map(
        local,
        mesh=mesh,
        in_specs=placed,
        out_specs=P(None, "prow", None, "pcol", None, None),
        check_vma=False,
    )
```

profile of v0, /device:TPU:1, one launch (start us, length us, event | category | flops | bytes accessed | tf_op | source)
XLA Modules:
  0.0 959.2 jit_solution(15155828020917416587)
XLA Ops:
  6.5 1.9 copy.15
  8.7 11.7 %cholesky.130 = f32[128,128]{1,0:T(8,128)S(1)} custom-call(f32[128,128]{1,0:T(8,128)S(1)} %cholesky.194), custom_call_target="Cholesky" | custom-call | tf_op jit(solution)/shard_map/jit(cholesky)/cholesky | solution.py:37
  20.5 9.8 %custom-call.13 = f32[1,128,128]{1,2,0:T(8,128)S(1)} custom-call(f32[1,128,128]{2,1,0:T(8,128)S(1)} %get-tuple-element.76), custom_call_target="InvertDiagBlocksLowerTriangular" | custom-call | tf_op jit(solution)/shard_map/jit(cholesky)/cholesky | solution.py:37
  30.5 0.3 convolution_subtract_fusion.3
  30.8 11.7 %cholesky.147 = f32[128,128]{1,0:T(8,128)S(1)} custom-call(f32[128,128]{1,0:T(8,128)S(1)} %convolution_subtract_fusion.3), custom_call_target="Cholesky" | custom-call | tf_op jit(solution)/shard_map/jit(cholesky)/cholesky | solution.py:37
  42.5 0.7 compare_reduce_fusion.2
  44.6 0.7 fusion.15
  45.3 0.4 all-reduce.10.cloned.1.call-start
  45.7 1.0 slice_bitcast_fusion.2
  46.8 1.6 copy.17
  48.4 116.4 %all-reduce.8.cloned.1.call-done = f32[256,256]{1,0:T(8,128)} async-done(((f32[256,256]{1,0:T(8,128)}), f32[256,256]{1,0:T(8,128)}) %all-reduce.8.cloned.1.call-update) | async-done | bytes 262160 | tf_op jit(solution)/shard_map/psum | solution.py:9
  164.8 1.0 fusion.14
  165.8 4.1 while.6
  165.8 0.6 fusion.39
  166.4 1.4 bitcast_dynamic-update-slice_fusion.6
  167.9 0.6 fusion.39
  168.5 1.4 bitcast_dynamic-update-slice_fusion.6
  169.9 0.6 copy-done.5
  170.6 20.5 %custom-call.14 = f32[2,128,128]{1,2,0:T(8,128)S(1)} custom-call(f32[2,128,128]{2,1,0:T(8,128)} %copy-done.5), custom_call_target="InvertDiagBlocksLowerTriangular" | custom-call | tf_op jit(solution)/shard_map/triangular_solve/custom-call.0 | solution.py:16
  191.1 0.6 fusion.6
  191.7 1.0 convolution_subtract_fusion.1
  192.7 0.6 fusion.21
  193.5 1.3 copy.18
  194.8 2.6 copy.19
  197.5 0.6 gather_fusion
  198.3 156.6 %all-reduce.10.cloned.1.call-done = f32[4,256,256]{1,2,0:T(8,128)} async-done(((f32[4,256,256]{1,2,0:T(8,128)}), f32[4,256,256]{1,2,0:T(8,128)}) %all-reduce.10.cloned.1.call-update) | async-done | bytes 1048592 | tf_op jit(solution)/shard_map/psum | solution.py:9
  354.9 1.4 broadcast_select_fusion.1
  356.2 1.4 gather_fusion.1
  357.6 1.9 select_select_fusion.2
  359.7 1.1 copy.23
  360.8 115.4 %all-reduce.12.cloned.1.call-done = f32[2,256,256]{1,2,0:T(8,128)} async-done(((f32[2,256,256]{1,2,0:T(8,128)}), f32[2,256,256]{1,2,0:T(8,128)}) %all-reduce.12.cloned.1.call-update) | async-done | bytes 524304 | tf_op jit(solution)/shard_map/psum | solution.py:9
  476.2 3.2 fusion.1
  479.4 1.3 copy-done
  481.2 11.7 %cholesky.164 = f32[128,128]{1,0:T(8,128)S(1)} custom-call(f32[128,128]{1,0:T(8,128)S(1)} %cholesky.197), custom_call_target="Cholesky" | custom-call | tf_op jit(solution)/shard_map/jit(cholesky)/cholesky | solution.py:37
  492.9 0.7 compare_reduce_fusion.1
  493.7 9.8 %custom-call.15 = f32[1,128,128]{1,2,0:T(8,128)S(1)} custom-call(f32[1,128,128]{2,1,0:T(8,128)S(1)} %get-tuple-element.72), custom_call_target="InvertDiagBlocksLowerTriangular" | custom-call | tf_op jit(solution)/shard_map/jit(cholesky)/cholesky | solution.py:37
  504.0 11.9 %cholesky.181 = f32[128,128]{1,0:T(8,128)S(1)} custom-call(f32[128,128]{1,0:T(8,128)S(1)} %convolution_subtract_fusion.2), custom_call_target="Cholesky" | custom-call | tf_op jit(solution)/shard_map/jit(cholesky)/cholesky | solution.py:37
  515.9 0.6 compare_reduce_fusion
  517.8 0.7 select_select_fusion.3
  518.6 0.3 copy.25
  518.9 114.4 %all-reduce.14.cloned.1.call-done = f32[256,256]{1,0:T(8,128)} async-done(((f32[256,256]{1,0:T(8,128)}), f32[256,256]{1,0:T(8,128)}) %all-reduce.14.cloned.1.call-update) | async-done | bytes 262160 | tf_op jit(solution)/shard_map/psum | solution.py:9
  633.3 1.0 fusion.12
  634.3 4.1 while.7
  634.4 0.6 fusion.40
  634.9 1.4 bitcast_dynamic-update-slice_fusion.7
  636.4 0.6 fusion.40
  637.0 1.4 bitcast_dynamic-update-slice_fusion.7
  638.4 19.7 %custom-call.16 = f32[2,128,128]{1,2,0:T(8,128)S(1)} custom-call(f32[2,128,128]{2,1,0:T(8,128)S(1)} %get-tuple-element.48), custom_call_target="InvertDiagBlocksLowerTriangular" | custom-call | tf_op jit(solution)/shard_map/triangular_solve/custom-call.0 | solution.py:16
  658.1 0.6 fusion.4
  658.7 1.0 convolution_subtract_fusion
  659.7 0.6 fusion.17
  660.5 1.3 copy.26
  661.8 2.6 copy.27
  664.5 0.6 slice.123
  665.1 0.6 fusion.26
  665.7 0.6 gather_fusion.2
  666.4 155.4 %all-reduce.16.cloned.1.call-done = f32[4,256,256]{1,2,0:T(8,128)} async-done(((f32[4,256,256]{1,2,0:T(8,128)}), f32[4,256,256]{1,2,0:T(8,128)}) %all-reduce.16.cloned.1.call-update) | async-done | bytes 1048592 | tf_op jit(solution)/shard_map/psum | solution.py:9
  821.8 2.4 broadcast_select_fusion
  824.2 2.6 gather_fusion.3
  826.9 2.0 select_select_fusion.1
  829.1 116.4 %all-reduce.18.cloned.1.call-done = f32[2,256,256]{1,2,0:T(8,128)} async-done(((f32[2,256,256]{1,2,0:T(8,128)}), f32[2,256,256]{1,2,0:T(8,128)}) %all-reduce.18.cloned.1.call-update) | async-done | bytes 524304 | tf_op jit(solution)/shard_map/psum | solution.py:9
  945.5 3.4 fusion
  949.1 1.1 copy-done.3
  950.4 1.8 copy.32
  (68 shorter events, 2.9 us)
Async XLA Ops:
  6.5 158.2 %all-reduce.8.cloned.1.call-start = ((), (), s32[]{:S(2)}) async-start(), calls=%async_computation | async-start | bytes 524288 | tf_op jit(solution)/shard_map/psum | solution.py:9
  8.7 38.1 %copy-start.6 = (s32[2,64]{1,0:T(2,128)S(1)}, s32[2,64]{1,0:T(2,128)}, u32[]{:S(2)}) copy-start(s32[2,64]{1,0:T(2,128)} %param.14) | copy-start | bytes 1540
  45.3 309.5 %all-reduce.10.cloned.1.call-start = ((), (), s32[]{:S(2)}) async-start(), calls=%async_computation.1 | async-start | bytes 2097152 | tf_op jit(solution)/shard_map/psum | solution.py:9
  169.9 0.7 copy-start.5
  197.4 278.8 %all-reduce.12.cloned.1.call-start = ((), (), s32[]{:S(2)}) async-start(), calls=%async_computation.2 | async-start | bytes 1048576 | tf_op jit(solution)/shard_map/psum | solution.py:9
  359.6 273.8 %all-reduce.14.cloned.1.call-start = ((), (), s32[]{:S(2)}) async-start(), calls=%async_computation.3 | async-start | bytes 524288 | tf_op jit(solution)/shard_map/psum | solution.py:9
  476.2 4.5 copy-start.2
  479.4 1.3 copy-start
  518.5 303.3 %all-reduce.16.cloned.1.call-start = ((), (), s32[]{:S(2)}) async-start(), calls=%async_computation.4 | async-start | bytes 2097152 | tf_op jit(solution)/shard_map/psum | solution.py:9
  664.4 281.1 %all-reduce.18.cloned.1.call-start = ((), (), s32[]{:S(2)}) async-start(), calls=%async_computation.5 | async-start | bytes 1048576 | tf_op jit(solution)/shard_map/psum | solution.py:9
  666.4 162.5 %copy-start.1 = (f32[4,2,256,256]{2,3,0,1:T(8,128)S(1)}, f32[4,2,256,256]{2,3,0,1:T(8,128)}, u32[]{:S(2)}) copy-start(f32[4,2,256,256]{2,3,0,1:T(8,128)} %copy-done) | copy-start | bytes 6291460
  826.8 2.1 copy-start.4
  948.9 1.2 copy-start.3
Sparse Core Ops, SparseCore 0:
  45.5 119.2 all-reduce.7
  197.6 157.2 all-reduce.9
  359.7 116.4 all-reduce.11
  518.7 114.6 all-reduce.13
  664.6 157.2 all-reduce.15
  829.0 116.4 all-reduce.17
where the time goes:
time: 968 us; the launch traced here: 959 us
  waiting for transfers between devices  775 us (80%)
  other arithmetic  122 us (13%)
  local copies, waits for them, and re-layouts  33.3 us (3%)
  between operations  16.7 us (2%)
  matrix products  12 us (1%)
    psum x6, waiting for transfers between devices, broadcast(): return lax.psum(block, axis)  775 us
    another operation x13, other arithmetic, local(): factor = broadcast(jnp.linalg.cholesky(local_diag), 'prow', column % nprow)  68.9 us
    another operation x5, other arithmetic, solve_blocks(): lax.linalg.triangular_solve(factor, right_hand, left_side=True, lower=True)  42.1 us
  transfers between devices with their start and end apart: 6, of which 6 were waited for; matrix products, arithmetic and copies ran while one was open for 1% of the time, Pallas kernels for 0%

commit v1 on v0

v1 whole, which is shorter than its diff:
```python
import jax
import jax.numpy as jnp
from jax import lax
from jax.experimental import pallas as pl
from jax.experimental.pallas import tpu as pltpu
from jax.sharding import PartitionSpec as P

B = 256
PANEL = 32
SUB = 8
LANES = 128
WINDOW = 3 * LANES
F32 = jnp.float32
BF16 = jnp.bfloat16


def split(x):
    high = x.astype(BF16)
    return high, (x - high.astype(F32)).astype(BF16)


def product(a, b, dims):
    dot = lambda x, y: lax.dot_general(x, y, (dims, ((), ())), preferred_element_type=F32)
    return dot(a[0], b[0]) + (dot(a[0], b[1]) + dot(a[1], b[0]))


NT = ((1,), (1,))
NN = ((1,), (0,))


def eliminate(work):
    spread = lambda x: jnp.broadcast_to(x, (SUB, LANES))
    sublane = lax.broadcasted_iota(jnp.int32, (SUB, WINDOW), 0)
    for top in range(0, B, PANEL):
        off = top // LANES * LANES
        groups = [work[top + SUB * q:top + SUB * (q + 1), off:off + WINDOW] for q in range(PANEL // SUB)]
        for g in range(PANEL // SUB):
            lane = top + SUB * g - off
            columns = [
                [spread(groups[q][:, lane + j:lane + j + 1]) for j in range(SUB)]
                for q in range(g, PANEL // SUB)
            ]
            s = [[spread(columns[0][j][i:i + 1, :]) for j in range(i + 1)] for i in range(SUB)]
            inverse = []
            for j in range(SUB):
                inverse.append(lax.rsqrt(s[j][j]))
                for i in range(j + 1, SUB):
                    s[i][j] = s[i][j] * inverse[j]
                for k in range(j + 1, SUB):
                    for i in range(k, SUB):
                        s[i][k] = s[i][k] - s[i][j] * s[k][j]
            wide = lambda x: jnp.concatenate([x] * (WINDOW // LANES), axis=1)
            rows = []
            result = None
            for j in range(SUB):
                row = jnp.broadcast_to(groups[g][j:j + 1, :], (SUB, WINDOW))
                for m in range(j):
                    row = row - wide(s[j][m]) * rows[m]
                row = row * wide(inverse[j])
                rows.append(row)
                result = row if result is None else jnp.where(sublane == j, row, result)
            groups[g] = result
            for q in range(g + 1, PANEL // SUB):
                cols = []
                total = groups[q]
                for j in range(SUB):
                    col = columns[q - g][j]
                    for m in range(j):
                        col = col - cols[m] * s[j][m]
                    col = col * inverse[j]
                    cols.append(col)
                    total = total - wide(col) * rows[j]
                groups[q] = total
        panel = jnp.concatenate(groups, axis=0)
        work[top:top + PANEL, off:off + WINDOW] = panel
        rest = top + PANEL
        if rest < B:
            start = rest // LANES * LANES
            left = split(panel[:, start - off:B - off].T)
            update = product(left, split(panel), NN)[rest - start:]
            work[rest:, off:off + WINDOW] = work[rest:, off:off + WINDOW] - update


def finish(work, factor_ref, inverse_ref):
    row = lax.broadcasted_iota(jnp.int32, (B, B), 0)
    col = lax.broadcasted_iota(jnp.int32, (B, B), 1)
    factor_ref[...] = jnp.where(col >= row, work[:, :B], 0.0).T
    inverse_ref[...] = work[:, B:]


def start(work, block):
    row = lax.broadcasted_iota(jnp.int32, (B, B), 0)
    col = lax.broadcasted_iota(jnp.int32, (B, B), 1)
    work[:, :B] = block
    work[:, B:] = jnp.where(row == col, 1.0, 0.0).astype(F32)


def first_kernel(block_ref, factor_ref, inverse_ref, work):
    start(work, block_ref[...])
    eliminate(work)
    finish(work, factor_ref, inverse_ref)


def second_kernel(flag_ref, pair_ref, w_ref, lower_ref, factor_ref, inverse_ref, work):
    lower = product(split(pair_ref[0]), split(w_ref[...]), NT)
    lower = jnp.where(flag_ref[0] > 0, lower, jnp.zeros_like(lower))
    lower_ref[...] = lower
    parts = split(lower)
    start(work, pair_ref[1] - product(parts, parts, NT))
    eliminate(work)
    finish(work, factor_ref, inverse_ref)


SQUARE = jax.ShapeDtypeStruct((B, B), F32)
ELIMINATION = pl.CostEstimate(flops=2 * B * B * B, bytes_accessed=24 << 20, transcendentals=0)


def factor_first(block):
    return pl.pallas_call(
        first_kernel,
        out_shape=(SQUARE, SQUARE),
        scratch_shapes=[pltpu.VMEM((B, 2 * B), F32)],
        cost_estimate=ELIMINATION,
        name="factor_first",
    )(block)


def factor_second(flag, pair, w):
    vmem = pl.BlockSpec(memory_space=pltpu.VMEM)
    return pl.pallas_call(
        second_kernel,
        out_shape=(SQUARE, SQUARE, SQUARE),
        in_specs=[pl.BlockSpec(memory_space=pltpu.SMEM), vmem, vmem],
        scratch_shapes=[pltpu.VMEM((B, 2 * B), F32)],
        cost_estimate=ELIMINATION,
        name="factor_second",
    )(flag, pair, w)


def panel_rows(first, second, flag0, flag1, w0, w1, lower):
    l0 = product(split(first), w0, NT)
    l0 = jnp.where(flag0, l0, jnp.zeros_like(l0))
    p0 = split(l0)
    l1 = product(split(second - product(p0, lower, NT)), w1, NT)
    l1 = jnp.where(flag1, l1, jnp.zeros_like(l1))
    return l0, l1, p0, split(l1)


def trailing_kernel(
    info, blocks_ref, rows_ref, cols_ref, w0_ref, w1_ref, lower_ref, g0_ref, g1_ref, out_ref,
    high0, low0, high1, low1, weights
):
    a = pl.program_id(0)
    count_c = high0.shape[0]
    count_r = pl.num_programs(0)

    @pl.when(a == 0)
    def _():
        for n, ref in enumerate((w0_ref, w1_ref, lower_ref)):
            weights[2 * n], weights[2 * n + 1] = split(ref[...])
        for b in range(count_c):
            flags = info[2 + 2 * count_r + b], info[2 + 2 * count_r + count_c + b]
            w0, w1, lower = ((weights[2 * n], weights[2 * n + 1]) for n in range(3))
            _, _, p0, p1 = panel_rows(
                cols_ref[0, b], cols_ref[1, b], flags[0] > 0, flags[1] > 0, w0, w1, lower
            )
            high0[b], low0[b] = p0
            high1[b], low1[b] = p1

    w0, w1, lower = ((weights[2 * n], weights[2 * n + 1]) for n in range(3))
    l0, l1, p0, p1 = panel_rows(
        rows_ref[0, 0], rows_ref[1, 0], info[2 + a] > 0, info[2 + count_r + a] > 0, w0, w1, lower
    )
    row = info[0] + info[2 + 2 * count_r + 2 * count_c] * a
    for b in range(count_c):
        col = info[1] + info[3 + 2 * count_r + 2 * count_c] * b
        old = blocks_ref[0, b]

        @pl.when(col > row)
        def _():
            out_ref[0, b] = old

        @pl.when(col == 0)
        def _():
            out_ref[0, b] = jnp.where(row == 0, g0_ref[...], l0)

        @pl.when((col == 1) & (row >= 1))
        def _():
            out_ref[0, b] = jnp.where(row == 1, g1_ref[...], l1)

        @pl.when((col > 1) & (col <= row))
        def _():
            update = product(p0, (high0[b], low0[b]), NT) + product(p1, (high1[b], low1[b]), NT)
            out_ref[0, b] = old - update


def trailing(info, blocks, rows, cols, w0, w1, lower, g0, g1):
    count_r, count_c = blocks.shape[0], blocks.shape[1]
    whole = lambda shape: pl.BlockSpec(shape, lambda a: (0,) * len(shape))
    own = pl.BlockSpec((1, count_c, B, B), lambda a: (a, 0, 0, 0))
    return pl.pallas_call(
        trailing_kernel,
        grid=(count_r,),
        out_shape=jax.ShapeDtypeStruct(blocks.shape, F32),
        in_specs=[
            pl.BlockSpec(memory_space=pltpu.SMEM),
            own,
            pl.BlockSpec((2, 1, B, B), lambda a: (0, a, 0, 0)),
            whole((2, count_c, B, B)),
        ] + [whole((B, B))] * 5,
        out_specs=own,
        scratch_shapes=[pltpu.VMEM((count_c, B, B), BF16)] * 4 + [pltpu.VMEM((6, B, B), BF16)],
        name="trailing",
    )(info, blocks, rows, cols, w0, w1, lower, g0, g1)


def local(stiffness, pattern):
    row_count, col_count = stiffness.shape[0], stiffness.shape[2]
    nprow, npcol = lax.axis_size("prow"), lax.axis_size("pcol")
    my_row, my_col = lax.axis_index("prow"), lax.axis_index("pcol")
    blocks = stiffness.reshape(row_count, col_count, B, B)
    both = ("prow", "pcol")
    only = lambda here, x: jnp.where(here, x, jnp.zeros_like(x))

    corner = blocks[0, 0]
    block00 = lax.psum(only((my_row == 0) & (my_col == 0), corner), both)
    pair = lax.psum(
        jnp.stack([only((my_row == 1) & (my_col == n), corner) for n in (0, 1)]), both
    )
    block00, pair, leading = lax.optimization_barrier((block00, pair, blocks[:, 0]))
    rows = lax.psum(jnp.stack([only(my_col == n, leading) for n in (0, 1)]), "pcol")
    g0, w0 = factor_first(block00)
    w0, rows = lax.optimization_barrier((w0, rows))

    glob_rows = my_row + nprow * jnp.arange(row_count, dtype=jnp.int32)
    glob_cols = my_col + npcol * jnp.arange(col_count, dtype=jnp.int32)
    wanted = jnp.take(rows, glob_cols // nprow, axis=1)
    cols = lax.psum(only(my_row == my_col % nprow, wanted), "prow")

    all_rows = jnp.arange(row_count * nprow, dtype=jnp.int32)
    flags0 = (pattern[0] == 1) & (all_rows > 0)
    flags1 = ((pattern[1] == 1) | flags0[1] & flags0) & (all_rows > 1)
    info = jnp.concatenate([
        jnp.stack([my_row, my_col]),
        jnp.take(flags0, glob_rows), jnp.take(flags1, glob_rows),
        jnp.take(flags0, glob_cols), jnp.take(flags1, glob_cols),
        jnp.array([nprow, npcol]),
    ]).astype(jnp.int32)

    lower, g1, w1 = factor_second(flags0[1:2].astype(jnp.int32), pair, w0)
    return trailing(info, blocks, rows, cols, w0, w1, lower, g0, g1).reshape(stiffness.shape)


def solution(mesh):
    placed = P(None, "prow", None, "pcol", None, None)
    return jax.shard_map(
        local, mesh=mesh, in_specs=(placed, P()), out_specs=placed, check_vma=False
    )
```

time: 968 us -> 589 us (0.61)
  waiting for transfers between devices: 775 us -> 529 us
  other arithmetic: 122 us -> 5.06 us
  Pallas kernels: 0 us -> 31.2 us
  local copies, waits for them, and re-layouts: 33.3 us -> 8.48 us
  matrix products: 12 us -> 0 us
    psum x6 -> x3, waiting for transfers between devices: 775 us -> 529 us  [the longest x1 280 us: local(): block00 = lax.psum(only((my_row == 0) & (my_col == 0), corner), both)]
    another operation x18 -> x3, other arithmetic: 111 us -> 2.47 us  [the longest x2 1.64 us: local(): jnp.stack([only(my_col == n, leading) for n in (0, 1)])]
    pallas_call x0 -> x3, Pallas kernels: none -> 31.2 us  [the longest x1 11.6 us: factor_second(): pl.pallas_call(second_kernel, out_shape=(SQUARE, SQUARE, SQUARE), in_spec...]
  transfers between devices with their start and end apart: 6 -> 3, of which waited for: 6 -> 3; matrix products, arithmetic and copies ran while one was open for 1% -> 1% of each run, Pallas kernels for 0% -> 4%
where the time goes in v1:
time: 589 us; the launch traced here: 588 us
  waiting for transfers between devices  529 us (90%)
  Pallas kernels  31.2 us (5%)
  between operations  13.8 us (2%)
  local copies, waits for them, and re-layouts  8.48 us (1%)
    psum x1, waiting for transfers between devices, local(): block00 = lax.psum(only((my_row == 0) & (my_col == 0), corner), both)  280 us
    psum x1, waiting for transfers between devices, local(): lax.psum(jnp.stack([only(my_col == n, leading) for n in (0, 1)]), 'pcol')  145 us
    psum x1, waiting for transfers between devices, local(): cols = lax.psum(only(my_row == my_col % nprow, wanted), 'prow')  104 us
  transfers between devices with their start and end apart: 3, of which 3 were waited for; matrix products, arithmetic and copies ran while one was open for 1% of the time, Pallas kernels for 4%

profile of v1, /device:TPU:1, one launch (start us, length us, event | category | flops | bytes accessed | tf_op | source)
XLA Modules:
  0.0 588.0 jit_solution(2656310744150741441)
XLA Ops:
  6.5 0.0 all-reduce.9.cloned.1.call-start
  6.5 1.8 copy.24
  8.4 0.7 fusion.3
  9.1 0.8 pad_maximum_fusion.1
  10.0 0.0 all-reduce.9.cloned.1.call-update
  10.0 0.0 all-reduce.5.cloned.1.call-start
  10.0 0.1 slice_bitcast_fusion
  10.1 279.7 %all-reduce.9.cloned.1.call-done = (f32[256,256]{1,0:T(8,128)}, f32[2,256,256]{2,1,0:T(8,128)}) async-done(((f32[256,256]{1,0:T(8,128)}, f32[2,256,256]{2,1,0:T(8,128)}), (f32[256,256]{1,0:T(8,128)}, f32[2,256,256]{2,1,0:T(8,128)})) %all-reduce.9.cloned.1.call-update) | async-done | bytes 786448 | tf_op jit(solution)/shard_map/psum | solution.py:226
  289.8 0.2 select_bitcast_fusion.1
  290.0 1.5 pad_maximum_fusion
  291.5 0.0 copy-start
  291.5 0.0 all-reduce.5.cloned.1.call-update
  291.5 0.0 all-reduce.7.cloned.1.call-start
  291.6 0.6 copy-done
  292.2 0.6 slice.18
  293.4 0.6 gather_fusion.3
  294.0 0.6 fusion.4
  294.6 0.6 gather_fusion.4
  295.3 10.5 %factor_first.1 = (f32[256,256]{1,0:T(8,128)}, f32[256,256]{1,0:T(8,128)}) custom-call(f32[256,256]{1,0:T(8,128)} %get-tuple-element.17.block_ref), custom_call_target="tpu_custom_call" | custom-call | flops 33554432 | bytes 25165824 | tf_op jit(solution)/shard_map/factor_first/pallas_call | solution.py:119
  305.8 145.4 %all-reduce.5.cloned.1.call-done.rows_ref = f32[2,4,256,256]{3,2,1,0:T(8,128)} async-done(((f32[2,4,256,256]{3,2,1,0:T(8,128)}), f32[2,4,256,256]{3,2,1,0:T(8,128)}) %all-reduce.5.cloned.1.call-update) | async-done | bytes 2097168 | tf_op jit(solution)/shard_map/psum | solution.py:231
  451.2 2.2 gather_fusion
  453.4 0.0 copy-start.1
  453.5 1.2 fusion.1
  454.6 0.0 all-reduce.7.cloned.1.call-update
  454.7 0.6 gather_fusion.2
  455.3 0.6 gather_fusion.1
  456.0 0.0 copy-done.1
  456.0 0.6 concatenate.3.info
  456.6 11.6 %factor_second.1 = (f32[256,256]{1,0:T(8,128)}, f32[256,256]{1,0:T(8,128)}, f32[256,256]{1,0:T(8,128)}) custom-call(s32[1]{0:T(128)S(6)} %convert_element_type.19.flag_ref, f32[2,256,256]{2,1,0:T(8,128)} %get-tuple-element.22.pair_ref, f32[256,256]{1,0:T(8,128)} %get-tuple-element.21.w_ref.w0_ref), custom_call_target="tpu_custom_call" | custom-call | flops 33554432 | bytes 25165824 | tf_op jit(solution)/shard_map/factor_second/pallas_call | solution.py:130
  468.2 104.1 %all-reduce.7.cloned.1.call-done.cols_ref = f32[2,2,256,256]{3,2,1,0:T(8,128)} async-done(((f32[2,2,256,256]{3,2,1,0:T(8,128)}), f32[2,2,256,256]{3,2,1,0:T(8,128)}) %all-reduce.7.cloned.1.call-update) | async-done | bytes 1048592 | tf_op jit(solution)/shard_map/psum | solution.py:238
  572.3 9.1 %trailing.1 = f32[4,2,256,256]{3,2,1,0:T(8,128)} custom-call(s32[16]{0:T(128)} %concatenate.3.info, f32[4,2,256,256]{3,2,1,0:T(8,128)} %bitcast.42, f32[2,4,256,256]{3,2,1,0:T(8,128)} %all-reduce.5.cloned.1.call-done.rows_ref, f32[2,2,256,256]{3,2,1,0:T(8,128)} %all-reduce.7.cloned.1.call-done.cols_ref, f32[256,256]{1,0:T(8,128)} %get-tuple-element.21.w_ref.w0_ref, ...), custom_call_target="tpu_custom_call" | custom-call | tf_op jit(solution)/shard_map/trailing/pallas_call | solution.py:201
  (11 shorter events, 0.1 us)
Async XLA Ops:
  6.5 283.3 %all-reduce.9.cloned.1.call-start = ((), (), s32[]{:S(2)}) async-start(), calls=%async_computation.2 | async-start | bytes 1572864 | tf_op jit(solution)/shard_map/psum | solution.py:226
  10.0 441.2 %all-reduce.5.cloned.1.call-start = ((), (), s32[]{:S(2)}) async-start(), calls=%async_computation | async-start | bytes 4194304 | tf_op jit(solution)/shard_map/psum | solution.py:231
  291.5 0.7 copy-start
  291.5 280.8 %all-reduce.7.cloned.1.call-start = ((), (), s32[]{:S(2)}) async-start(), calls=%async_computation.1 | async-start | bytes 2097152 | tf_op jit(solution)/shard_map/psum | solution.py:238
  453.4 2.5 copy-start.1
Sparse Core Ops, SparseCore 0:
  12.5 277.2 all-reduce.8
  293.4 157.8 all-reduce.4
  454.8 117.5 all-reduce.6

commit v2 on v1

--- a/solution.py
+++ b/solution.py
@@ -214,29 +214,216 @@
     )(info, blocks, rows, cols, w0, w1, lower, g0, g1)
 
 
+CHIPS_X, CHIPS_Y, CHIPS_Z = 4, 8, 8
+PIECES = 8
+MESH = pl.DeviceIdType.MESH
+
+
+def spread_kernel(
+    lead, rows, cols, corner, x_send, x_recv, z_send, z_recv, y_send, y_recv, core_send, core_recv, here
+):
+    prow, pcol = lax.axis_index("prow"), lax.axis_index("pcol")
+    y, core = prow // 2, prow % 2
+    z, x = pcol // CHIPS_X, pcol % CHIPS_X
+    order = lead.shape[1]
+    piece = order * 4 // (2 * PIECES)
+
+    def at_x(step):
+        return {"pcol": z * CHIPS_X + (x + step + CHIPS_X) % CHIPS_X}
+
+    def at_z(step):
+        return {"pcol": (z + step + CHIPS_Z) % CHIPS_Z * CHIPS_X + x}
+
+    def at_y(step):
+        return {"prow": (y + step + CHIPS_Y) % CHIPS_Y * 2 + core}
+
+    partner = {"prow": y * 2 + 1 - core}
+    neighbours = [at(step) for at in (at_x, at_z, at_y) for step in (1, -1)] + [partner]
+    barrier = pltpu.get_barrier_semaphore()
+    for device in neighbours:
+        pl.semaphore_signal(barrier, inc=1, device_id=device, device_id_type=MESH)
+    pl.semaphore_wait(barrier, len(neighbours))
+
+    def remote(ref, send, recv, device):
+        return pltpu.make_async_remote_copy(
+            src_ref=ref, dst_ref=ref, send_sem=send, recv_sem=recv, device_id=device, device_id_type=MESH
+        )
+
+    for n in (0, 1):
+        @pl.when(pcol == n)
+        def _():
+            copy = pltpu.make_async_copy(lead, rows.at[n], here)
+            copy.start()
+            copy.wait()
+
+    streams = []
+    for n in (0, 1):
+        for h in (0, 1):
+            in_x = (x + CHIPS_X - n) % CHIPS_X if h == 0 else (n + CHIPS_X - x) % CHIPS_X
+            in_z = z if h == 0 else (CHIPS_Z - z) % CHIPS_Z
+            streams.append((n, h, in_x, in_z))
+    deepest = streams[0][2] + streams[0][3]
+    for _, _, in_x, in_z in streams[1:]:
+        deepest = jnp.maximum(deepest, in_x + in_z)
+
+    def row_copies(n, h, p):
+        per = 2 * piece * (PIECES // 4) // 2
+        first = pl.multiple_of(h * per + p % (PIECES // 4) * piece, piece)
+        ref = rows.at[n, p // (PIECES // 4), pl.ds(first, piece)]
+        k = (n * 2 + h) * PIECES + p
+        step = 1 if h == 0 else -1
+        return (
+            remote(ref, x_send.at[k], x_recv.at[k], at_x(step)),
+            remote(ref, z_send.at[k], z_recv.at[k], at_z(step)),
+        )
+
+    half_order = order // 2
+    items = []
+    for q in range(3):
+        for k in (0, 1):
+            part = pl.ds(k * half_order, half_order)
+            source = min(q, 1)
+            items.append((deepest + 2 + 2 * q + k, source, rows.at[q // 2, 0, part], corner.at[q, part]))
+    wanted = pcol // (2 * CHIPS_Y)
+    for b in (0, 1):
+        for n in (0, 1):
+            for k in (0, 1):
+                part = pl.ds(k * half_order, half_order)
+                when = deepest + (PIECES // 2 + 2 if b == 0 else PIECES) + 2 * n + k
+                items.append(
+                    (when, pcol % (2 * CHIPS_Y), rows.at[n, wanted + 2 * b, part], cols.at[n, b, part])
+                )
+    far = CHIPS_Y // 2
+
+    def item_copies(k, ref):
+        return (
+            remote(ref, y_send.at[2 * k], y_recv.at[k], at_y(1)),
+            remote(ref, y_send.at[2 * k + 1], y_recv.at[k], at_y(-1)),
+            remote(ref, core_send.at[k], core_recv.at[k], partner),
+        )
+
+    def place(source):
+        ahead = (y + CHIPS_Y - source // 2) % CHIPS_Y
+        up = ahead < far
+        down = (ahead == 0) | (ahead > far + 1) if CHIPS_Y > 2 else ahead < 0
+        return ahead, jnp.minimum(ahead, CHIPS_Y - ahead), up, down
+
+    def step(t, carry):
+        for n, h, in_x, in_z in streams:
+            p = t - in_x - in_z
+
+            @pl.when((p >= 0) & (p < PIECES))
+            def _():
+                along_x, along_z = row_copies(n, h, p)
+
+                @pl.when((in_z == 0) & (in_x > 0))
+                def _():
+                    along_x.wait_recv()
+
+                @pl.when(in_z > 0)
+                def _():
+                    along_z.wait_recv()
+
+                @pl.when((in_z == 0) & (in_x < CHIPS_X - 1))
+                def _():
+                    along_x.start()
+
+                @pl.when(in_z < CHIPS_Z - 1)
+                def _():
+                    along_z.start()
+
+        for k, (when, source, origin, ref) in enumerate(items):
+            ahead, depth, up, down = place(source)
+            above, below, across = item_copies(k, ref)
+
+            @pl.when((t == when + depth) & (core == source % 2))
+            def _():
+                @pl.when(ahead == 0)
+                def _():
+                    copy = pltpu.make_async_copy(origin, ref, here)
+                    copy.start()
+                    copy.wait()
+
+                @pl.when(ahead > 0)
+                def _():
+                    above.wait_recv()
+
+                @pl.when(up)
+                def _():
+                    above.start()
+
+                @pl.when(down)
+                def _():
+                    below.start()
+
+                across.start()
+
+            @pl.when((t == when + depth + 1) & (core != source % 2))
+            def _():
+                across.wait_recv()
+
+        return carry
+
+    steps = CHIPS_X + CHIPS_Z - 2 + PIECES + 4 + far + 2
+    lax.fori_loop(0, steps, step, 0)
+
+    def drain(p, carry):
+        for n, h, in_x, in_z in streams:
+            along_x, along_z = row_copies(n, h, p)
+
+            @pl.when((in_z == 0) & (in_x < CHIPS_X - 1))
+            def _():
+                along_x.wait_send()
+
+            @pl.when(in_z < CHIPS_Z - 1)
+            def _():
+                along_z.wait_send()
+
+        return carry
+
+    lax.fori_loop(0, PIECES, drain, 0)
+    for k, (_, source, _, ref) in enumerate(items):
+        _, _, up, down = place(source)
+        above, below, across = item_copies(k, ref)
+
+        @pl.when(core == source % 2)
+        def _():
+            @pl.when(up)
+            def _():
+                above.wait_send()
+
+            @pl.when(down)
+            def _():
+                below.wait_send()
+
+            across.wait_send()
+
+
+def spread(lead):
+    count, order = lead.shape[0], lead.shape[1]
+    vmem = pl.BlockSpec(memory_space=pltpu.VMEM)
+    shapes = ((2, count, order, order), (2, 2, order, order), (3, order, order))
+    dma = pltpu.SemaphoreType.DMA
+    return pl.pallas_call(
+        spread_kernel,
+        out_shape=tuple(jax.ShapeDtypeStruct(shape, F32) for shape in shapes),
+        in_specs=[vmem],
+        out_specs=(vmem,) * 3,
+        scratch_shapes=[dma((4 * PIECES,))] * 4 + [dma((28,)), dma((14,)), dma((14,)), dma((14,)), dma(())],
+        compiler_params=pltpu.CompilerParams(collective_id=0, has_side_effects=True),
+        name="spread",
+    )(lead)
+
+
 def local(stiffness, pattern):
     row_count, col_count = stiffness.shape[0], stiffness.shape[2]
     nprow, npcol = lax.axis_size("prow"), lax.axis_size("pcol")
     my_row, my_col = lax.axis_index("prow"), lax.axis_index("pcol")
     blocks = stiffness.reshape(row_count, col_count, B, B)
-    both = ("prow", "pcol")
-    only = lambda here, x: jnp.where(here, x, jnp.zeros_like(x))
-
-    corner = blocks[0, 0]
-    block00 = lax.psum(only((my_row == 0) & (my_col == 0), corner), both)
-    pair = lax.psum(
-        jnp.stack([only((my_row == 1) & (my_col == n), corner) for n in (0, 1)]), both
-    )
-    block00, pair, leading = lax.optimization_barrier((block00, pair, blocks[:, 0]))
-    rows = lax.psum(jnp.stack([only(my_col == n, leading) for n in (0, 1)]), "pcol")
-    g0, w0 = factor_first(block00)
-    w0, rows = lax.optimization_barrier((w0, rows))
-
+    rows, cols, corner = spread(blocks[:, 0])
+    g0, w0 = factor_first(corner[0])
     glob_rows = my_row + nprow * jnp.arange(row_count, dtype=jnp.int32)
     glob_cols = my_col + npcol * jnp.arange(col_count, dtype=jnp.int32)
-    wanted = jnp.take(rows, glob_cols // nprow, axis=1)
-    cols = lax.psum(only(my_row == my_col % nprow, wanted), "prow")
-
     all_rows = jnp.arange(row_count * nprow, dtype=jnp.int32)
     flags0 = (pattern[0] == 1) & (all_rows > 0)
     flags1 = ((pattern[1] == 1) | flags0[1] & flags0) & (all_rows > 1)
@@ -247,7 +434,7 @@
         jnp.array([nprow, npcol]),
     ]).astype(jnp.int32)
 
-    lower, g1, w1 = factor_second(flags0[1:2].astype(jnp.int32), pair, w0)
+    lower, g1, w1 = factor_second(flags0[1:2].astype(jnp.int32), corner[1:], w0)
     return trailing(info, blocks, rows, cols, w0, w1, lower, g0, g1).reshape(stiffness.shape)
 
 

time: 589 us -> 153 us (0.26)
  the two profiles are of different devices: /device:TPU:1 before, /device:TPU:125 now
where the time goes in v2:
time: 153 us
  Pallas kernels  142 us (93%)
  local copies, waits for them, and re-layouts  8.41 us (5%)
  other arithmetic  2.2 us (1%)
    pallas_call x1, Pallas kernels, spread(): pl.pallas_call(spread_kernel, out_shape=tuple((jax.ShapeDtypeStruct(shape...  109 us
    pallas_call x1, Pallas kernels, factor_second(): pl.pallas_call(second_kernel, out_shape=(SQUARE, SQUARE, SQUARE), in_spec...  11.6 us
    pallas_call x1, Pallas kernels, factor_first(): pl.pallas_call(first_kernel, out_shape=(SQUARE, SQUARE), scratch_shapes=[...  10.5 us
    pallas_call x1, Pallas kernels, trailing(): pl.pallas_call(trailing_kernel, grid=(count_r,), out_shape=jax.ShapeDtype...  10.2 us

profile of v2, /device:TPU:125, one launch (start us, length us, event | category | flops | bytes accessed | tf_op | source)
XLA Modules:
  0.0 152.8 jit_solution(6295205669766120610)
XLA Ops:
  0.0 0.0 copy-start.1
  0.0 0.0 copy-start
  0.0 0.8 bitcast_and_fusion
  0.8 0.6 slice.21
  2.0 1.3 fusion
  3.3 0.6 gather_fusion.3
  4.0 0.6 gather_fusion.2
  4.6 0.6 gather_fusion.1
  5.3 0.6 gather_fusion
  5.9 0.0 copy-done.1
  5.9 0.7 concatenate.3.info
  6.6 0.0 copy-done
  6.6 1.0 slice_bitcast_fusion.lead
  7.7 109.2 %spread.1 = (f32[2,4,256,256]{3,2,1,0:T(8,128)}, f32[2,2,256,256]{3,2,1,0:T(8,128)}, f32[3,256,256]{2,1,0:T(8,128)}) custom-call(f32[4,256,256]{2,1,0:T(8,128)} %slice_bitcast_fusion.lead), custom_call_target="tpu_custom_call" | custom-call | tf_op jit(solution)/shard_map/spread/pallas_call | solution.py:407
  116.9 1.7 %slice_bitcast_fusion.1.block_ref = f32[256,256]{1,0:T(8,128)} fusion(f32[3,256,256]{2,1,0:T(8,128)} %get-tuple-element.17), kind=kLoop, calls=%fused_computation.5 | loop fusion | bytes 524288 | tf_op jit(solution)/shard_map/squeeze | solution.py:424
  118.6 1.9 %slice.24.pair_ref = f32[2,256,256]{2,1,0:T(8,128)} slice(f32[3,256,256]{2,1,0:T(8,128)} %get-tuple-element.17), slice={[1:3], [0:256], [0:256]} | slice | bytes 1048576 | tf_op jit(solution)/shard_map/slice | solution.py:437
  120.4 10.5 %factor_first.1 = (f32[256,256]{1,0:T(8,128)}, f32[256,256]{1,0:T(8,128)}) custom-call(f32[256,256]{1,0:T(8,128)} %slice_bitcast_fusion.1.block_ref), custom_call_target="tpu_custom_call" | custom-call | flops 33554432 | bytes 25165824 | tf_op jit(solution)/shard_map/factor_first/pallas_call | solution.py:119
  131.0 11.6 %factor_second.1 = (f32[256,256]{1,0:T(8,128)}, f32[256,256]{1,0:T(8,128)}, f32[256,256]{1,0:T(8,128)}) custom-call(s32[1]{0:T(128)S(6)} %convert_element_type.19.flag_ref, f32[2,256,256]{2,1,0:T(8,128)} %slice.24.pair_ref, f32[256,256]{1,0:T(8,128)} %get-tuple-element.18.w_ref.w0_ref), custom_call_target="tpu_custom_call" | custom-call | flops 33554432 | bytes 25165824 | tf_op jit(solution)/shard_map/factor_second/pallas_call | solution.py:130
  142.5 10.2 %trailing.1 = f32[4,2,256,256]{3,2,1,0:T(8,128)} custom-call(s32[16]{0:T(128)} %concatenate.3.info, f32[4,2,256,256]{3,2,1,0:T(8,128)} %bitcast.19, f32[2,4,256,256]{3,2,1,0:T(8,128)} %get-tuple-element.15.rows_ref, f32[2,2,256,256]{3,2,1,0:T(8,128)} %get-tuple-element.16.cols_ref, f32[256,256]{1,0:T(8,128)} %get-tuple-element.18.w_ref.w0_ref, ...), custom_call_target="tpu_custom_call" | custom-call | tf_op jit(solution)/shard_map/trailing/pallas_call | solution.py:201
  (6 shorter events, 0.0 us)
Async XLA Ops:
  0.0 5.9 %copy-start.1 = (s32[2]{0:T(128)S(1)}, s32[2]{0:T(128)}, u32[]{:S(2)}) copy-start(s32[2]{0:T(128)} %constant.10.clone) | copy-start | bytes 28
  0.0 6.6 %copy-start = (f32[4,1,2,1,256,256]{5,4,3,2,1,0:T(8,128)S(1)}, f32[4,1,2,1,256,256]{5,4,3,2,1,0:T(8,128)}, u32[]{:S(2)}) copy-start(f32[4,1,2,1,256,256]{5,4,3,2,1,0:T(8,128)} %param.7) | copy-start | bytes 6291460

commit v3 on v2

--- a/solution.py
+++ b/solution.py
@@ -95,18 +95,18 @@
     work[:, B:] = jnp.where(row == col, 1.0, 0.0).astype(F32)
 
 
-def first_kernel(block_ref, factor_ref, inverse_ref, work):
-    start(work, block_ref[...])
+def first_kernel(corner_ref, factor_ref, inverse_ref, work):
+    start(work, corner_ref[0])
     eliminate(work)
     finish(work, factor_ref, inverse_ref)
 
 
-def second_kernel(flag_ref, pair_ref, w_ref, lower_ref, factor_ref, inverse_ref, work):
-    lower = product(split(pair_ref[0]), split(w_ref[...]), NT)
-    lower = jnp.where(flag_ref[0] > 0, lower, jnp.zeros_like(lower))
+def second_kernel(pattern, corner_ref, w_ref, lower_ref, factor_ref, inverse_ref, work):
+    lower = product(split(corner_ref[1]), split(w_ref[...]), NT)
+    lower = jnp.where(pattern[0, 1] == 1, lower, jnp.zeros_like(lower))
     lower_ref[...] = lower
     parts = split(lower)
-    start(work, pair_ref[1] - product(parts, parts, NT))
+    start(work, corner_ref[2] - product(parts, parts, NT))
     eliminate(work)
     finish(work, factor_ref, inverse_ref)
 
@@ -115,17 +115,17 @@
 ELIMINATION = pl.CostEstimate(flops=2 * B * B * B, bytes_accessed=24 << 20, transcendentals=0)
 
 
-def factor_first(block):
+def factor_first(corner):
     return pl.pallas_call(
         first_kernel,
         out_shape=(SQUARE, SQUARE),
         scratch_shapes=[pltpu.VMEM((B, 2 * B), F32)],
         cost_estimate=ELIMINATION,
         name="factor_first",
-    )(block)
-
-
-def factor_second(flag, pair, w):
+    )(corner)
+
+
+def factor_second(pattern, corner, w):
     vmem = pl.BlockSpec(memory_space=pltpu.VMEM)
     return pl.pallas_call(
         second_kernel,
@@ -134,7 +134,7 @@
         scratch_shapes=[pltpu.VMEM((B, 2 * B), F32)],
         cost_estimate=ELIMINATION,
         name="factor_second",
-    )(flag, pair, w)
+    )(pattern, corner, w)
 
 
 def panel_rows(first, second, flag0, flag1, w0, w1, lower):
@@ -147,33 +147,36 @@
 
 
 def trailing_kernel(
-    info, blocks_ref, rows_ref, cols_ref, w0_ref, w1_ref, lower_ref, g0_ref, g1_ref, out_ref,
+    pattern, blocks_ref, rows_ref, cols_ref, w0_ref, w1_ref, lower_ref, g0_ref, g1_ref, out_ref,
     high0, low0, high1, low1, weights
 ):
     a = pl.program_id(0)
     count_c = high0.shape[0]
-    count_r = pl.num_programs(0)
+    prow, pcol = lax.axis_index("prow"), lax.axis_index("pcol")
+    nprow, npcol = lax.axis_size("prow"), lax.axis_size("pcol")
+
+    def flags(i):
+        first = (pattern[0, i] == 1) & (i > 0)
+        return first, ((pattern[1, i] == 1) | ((pattern[0, 1] == 1) & first)) & (i > 1)
+
 
     @pl.when(a == 0)
     def _():
         for n, ref in enumerate((w0_ref, w1_ref, lower_ref)):
             weights[2 * n], weights[2 * n + 1] = split(ref[...])
         for b in range(count_c):
-            flags = info[2 + 2 * count_r + b], info[2 + 2 * count_r + count_c + b]
             w0, w1, lower = ((weights[2 * n], weights[2 * n + 1]) for n in range(3))
             _, _, p0, p1 = panel_rows(
-                cols_ref[0, b], cols_ref[1, b], flags[0] > 0, flags[1] > 0, w0, w1, lower
+                cols_ref[0, b].T, cols_ref[1, b].T, *flags(pcol + npcol * b), w0, w1, lower
             )
             high0[b], low0[b] = p0
             high1[b], low1[b] = p1
 
     w0, w1, lower = ((weights[2 * n], weights[2 * n + 1]) for n in range(3))
-    l0, l1, p0, p1 = panel_rows(
-        rows_ref[0, 0], rows_ref[1, 0], info[2 + a] > 0, info[2 + count_r + a] > 0, w0, w1, lower
-    )
-    row = info[0] + info[2 + 2 * count_r + 2 * count_c] * a
+    row = prow + nprow * a
+    l0, l1, p0, p1 = panel_rows(rows_ref[0, 0], rows_ref[1, 0], *flags(row), w0, w1, lower)
     for b in range(count_c):
-        col = info[1] + info[3 + 2 * count_r + 2 * count_c] * b
+        col = pcol + npcol * b
         old = blocks_ref[0, b]
 
         @pl.when(col > row)
@@ -194,7 +197,7 @@
             out_ref[0, b] = old - update
 
 
-def trailing(info, blocks, rows, cols, w0, w1, lower, g0, g1):
+def trailing(pattern, blocks, rows, cols, w0, w1, lower, g0, g1):
     count_r, count_c = blocks.shape[0], blocks.shape[1]
     whole = lambda shape: pl.BlockSpec(shape, lambda a: (0,) * len(shape))
     own = pl.BlockSpec((1, count_c, B, B), lambda a: (a, 0, 0, 0))
@@ -211,21 +214,21 @@
         out_specs=own,
         scratch_shapes=[pltpu.VMEM((count_c, B, B), BF16)] * 4 + [pltpu.VMEM((6, B, B), BF16)],
         name="trailing",
-    )(info, blocks, rows, cols, w0, w1, lower, g0, g1)
+    )(pattern, blocks, rows, cols, w0, w1, lower, g0, g1)
 
 
 CHIPS_X, CHIPS_Y, CHIPS_Z = 4, 8, 8
-PIECES = 8
+PIECES = 32
 MESH = pl.DeviceIdType.MESH
 
 
 def spread_kernel(
-    lead, rows, cols, corner, x_send, x_recv, z_send, z_recv, y_send, y_recv, core_send, core_recv, here
+    blocks, rows, cols, corner, x_send, x_recv, z_send, z_recv, y_send, y_recv, core_send, core_recv, here
 ):
     prow, pcol = lax.axis_index("prow"), lax.axis_index("pcol")
     y, core = prow // 2, prow % 2
     z, x = pcol // CHIPS_X, pcol % CHIPS_X
-    order = lead.shape[1]
+    order = blocks.shape[2]
     piece = order * 4 // (2 * PIECES)
 
     def at_x(step):
@@ -252,7 +255,7 @@
     for n in (0, 1):
         @pl.when(pcol == n)
         def _():
-            copy = pltpu.make_async_copy(lead, rows.at[n], here)
+            copy = pltpu.make_async_copy(blocks.at[:, 0], rows.at[n], here)
             copy.start()
             copy.wait()
 
@@ -283,16 +286,13 @@
         for k in (0, 1):
             part = pl.ds(k * half_order, half_order)
             source = min(q, 1)
-            items.append((deepest + 2 + 2 * q + k, source, rows.at[q // 2, 0, part], corner.at[q, part]))
-    wanted = pcol // (2 * CHIPS_Y)
+            when = deepest + PIECES // 4 + 2 * q + k
+            items.append((when, source, rows.at[q // 2, 0, part], corner.at[q, part]))
     for b in (0, 1):
-        for n in (0, 1):
-            for k in (0, 1):
-                part = pl.ds(k * half_order, half_order)
-                when = deepest + (PIECES // 2 + 2 if b == 0 else PIECES) + 2 * n + k
-                items.append(
-                    (when, pcol % (2 * CHIPS_Y), rows.at[n, wanted + 2 * b, part], cols.at[n, b, part])
-                )
+        for k in (0, 1):
+            part = pl.ds(k * half_order, half_order)
+            for n in (0, 1):
+                items.append((2 * (2 * b + k), n, blocks.at[0, b, part], cols.at[n, b, part]))
     far = CHIPS_Y // 2
 
     def item_copies(k, ref):
@@ -336,7 +336,7 @@
             ahead, depth, up, down = place(source)
             above, below, across = item_copies(k, ref)
 
-            @pl.when((t == when + depth) & (core == source % 2))
+            @pl.when((t == when + 2 * depth) & (core == source % 2))
             def _():
                 @pl.when(ahead == 0)
                 def _():
@@ -358,13 +358,13 @@
 
                 across.start()
 
-            @pl.when((t == when + depth + 1) & (core != source % 2))
+            @pl.when((t == when + 2 * depth + 2) & (core != source % 2))
             def _():
                 across.wait_recv()
 
         return carry
 
-    steps = CHIPS_X + CHIPS_Z - 2 + PIECES + 4 + far + 2
+    steps = CHIPS_X + CHIPS_Z - 2 + PIECES + 2 * far + 8
     lax.fori_loop(0, steps, step, 0)
 
     def drain(p, carry):
@@ -399,43 +399,28 @@
             across.wait_send()
 
 
-def spread(lead):
-    count, order = lead.shape[0], lead.shape[1]
+def spread(blocks):
+    count, order = blocks.shape[0], blocks.shape[2]
     vmem = pl.BlockSpec(memory_space=pltpu.VMEM)
     shapes = ((2, count, order, order), (2, 2, order, order), (3, order, order))
     dma = pltpu.SemaphoreType.DMA
     return pl.pallas_call(
         spread_kernel,
         out_shape=tuple(jax.ShapeDtypeStruct(shape, F32) for shape in shapes),
-        in_specs=[vmem],
+        in_specs=[pl.BlockSpec(memory_space=pl.ANY)],
         out_specs=(vmem,) * 3,
         scratch_shapes=[dma((4 * PIECES,))] * 4 + [dma((28,)), dma((14,)), dma((14,)), dma((14,)), dma(())],
         compiler_params=pltpu.CompilerParams(collective_id=0, has_side_effects=True),
         name="spread",
-    )(lead)
+    )(blocks)
 
 
 def local(stiffness, pattern):
-    row_count, col_count = stiffness.shape[0], stiffness.shape[2]
-    nprow, npcol = lax.axis_size("prow"), lax.axis_size("pcol")
-    my_row, my_col = lax.axis_index("prow"), lax.axis_index("pcol")
-    blocks = stiffness.reshape(row_count, col_count, B, B)
-    rows, cols, corner = spread(blocks[:, 0])
-    g0, w0 = factor_first(corner[0])
-    glob_rows = my_row + nprow * jnp.arange(row_count, dtype=jnp.int32)
-    glob_cols = my_col + npcol * jnp.arange(col_count, dtype=jnp.int32)
-    all_rows = jnp.arange(row_count * nprow, dtype=jnp.int32)
-    flags0 = (pattern[0] == 1) & (all_rows > 0)
-    flags1 = ((pattern[1] == 1) | flags0[1] & flags0) & (all_rows > 1)
-    info = jnp.concatenate([
-        jnp.stack([my_row, my_col]),
-        jnp.take(flags0, glob_rows), jnp.take(flags1, glob_rows),
-        jnp.take(flags0, glob_cols), jnp.take(flags1, glob_cols),
-        jnp.array([nprow, npcol]),
-    ]).astype(jnp.int32)
-
-    lower, g1, w1 = factor_second(flags0[1:2].astype(jnp.int32), corner[1:], w0)
-    return trailing(info, blocks, rows, cols, w0, w1, lower, g0, g1).reshape(stiffness.shape)
+    blocks = stiffness.reshape(stiffness.shape[0], stiffness.shape[2], B, B)
+    rows, cols, corner = spread(blocks)
+    g0, w0 = factor_first(corner)
+    lower, g1, w1 = factor_second(pattern, corner, w0)
+    return trailing(pattern, blocks, rows, cols, w0, w1, lower, g0, g1).reshape(stiffness.shape)
 
 
 def solution(mesh):

time: 153 us -> 165 us (1.078)
  the two profiles are of different devices: /device:TPU:125 before, /device:TPU:92 now
where the time goes in v3:
time: 165 us
  Pallas kernels  165 us (100%)
    pallas_call x1, Pallas kernels, spread(): pl.pallas_call(spread_kernel, out_shape=tuple((jax.ShapeDtypeStruct(shape...  132 us
    pallas_call x1, Pallas kernels, factor_second(): pl.pallas_call(second_kernel, out_shape=(SQUARE, SQUARE, SQUARE), in_spec...  11.7 us
    pallas_call x1, Pallas kernels, factor_first(): pl.pallas_call(first_kernel, out_shape=(SQUARE, SQUARE), scratch_shapes=[...  10.7 us
    pallas_call x1, Pallas kernels, trailing(): pl.pallas_call(trailing_kernel, grid=(count_r,), out_shape=jax.ShapeDtype...  10.3 us

profile of v3, /device:TPU:92, one launch (start us, length us, event | category | flops | bytes accessed | tf_op | source)
XLA Modules:
  0.0 165.0 jit_solution(16326241463300720241)
XLA Ops:
  0.0 132.3 %spread.1 = (f32[2,4,256,256]{3,2,1,0:T(8,128)}, f32[2,2,256,256]{3,2,1,0:T(8,128)}, f32[3,256,256]{2,1,0:T(8,128)}) custom-call(f32[4,2,256,256]{3,2,1,0:T(8,128)} %bitcast.4), custom_call_target="tpu_custom_call" | custom-call | tf_op jit(solution)/shard_map/spread/pallas_call | solution.py:407
  132.3 10.7 %factor_first.1 = (f32[256,256]{1,0:T(8,128)}, f32[256,256]{1,0:T(8,128)}) custom-call(f32[3,256,256]{2,1,0:T(8,128)} %get-tuple-element.15.corner_ref), custom_call_target="tpu_custom_call" | custom-call | flops 33554432 | bytes 25165824 | tf_op jit(solution)/shard_map/factor_first/pallas_call | solution.py:119
  143.0 11.7 %factor_second.1 = (f32[256,256]{1,0:T(8,128)}, f32[256,256]{1,0:T(8,128)}, f32[256,256]{1,0:T(8,128)}) custom-call(s32[2,64]{1,0:T(2,128)} %pattern.3, f32[3,256,256]{2,1,0:T(8,128)} %get-tuple-element.15.corner_ref, f32[256,256]{1,0:T(8,128)} %get-tuple-element.16.w_ref.w0_ref), custom_call_target="tpu_custom_call" | custom-call | flops 33554432 | bytes 25165824 | tf_op jit(solution)/shard_map/factor_second/pallas_call | solution.py:130
  154.7 10.3 %trailing.1 = f32[4,2,256,256]{3,2,1,0:T(8,128)} custom-call(s32[2,64]{1,0:T(2,128)} %pattern.3, f32[4,2,256,256]{3,2,1,0:T(8,128)} %bitcast.5, f32[2,4,256,256]{3,2,1,0:T(8,128)} %get-tuple-element.13.rows_ref, f32[2,2,256,256]{3,2,1,0:T(8,128)} %get-tuple-element.14.cols_ref, f32[256,256]{1,0:T(8,128)} %get-tuple-element.16.w_ref.w0_ref, ...), custom_call_target="tpu_custom_call" | custom-call | tf_op jit(solution)/shard_map/trailing/pallas_call | solution.py:204

commit v4 on v3

--- a/solution.py
+++ b/solution.py
@@ -218,7 +218,8 @@
 
 
 CHIPS_X, CHIPS_Y, CHIPS_Z = 4, 8, 8
-PIECES = 32
+PIECES = 16
+HOP = 2
 MESH = pl.DeviceIdType.MESH
 
 
@@ -241,7 +242,8 @@
         return {"prow": (y + step + CHIPS_Y) % CHIPS_Y * 2 + core}
 
     partner = {"prow": y * 2 + 1 - core}
-    neighbours = [at(step) for at in (at_x, at_z, at_y) for step in (1, -1)] + [partner]
+    sides_x, sides_y, sides_z = ({step: at(step) for step in (1, -1)} for at in (at_x, at_y, at_z))
+    neighbours = [sides[step] for sides in (sides_x, sides_z, sides_y) for step in (1, -1)] + [partner]
     barrier = pltpu.get_barrier_semaphore()
     for device in neighbours:
         pl.semaphore_signal(barrier, inc=1, device_id=device, device_id_type=MESH)
@@ -276,8 +278,8 @@
         k = (n * 2 + h) * PIECES + p
         step = 1 if h == 0 else -1
         return (
-            remote(ref, x_send.at[k], x_recv.at[k], at_x(step)),
-            remote(ref, z_send.at[k], z_recv.at[k], at_z(step)),
+            remote(ref, x_send.at[k], x_recv.at[k], sides_x[step]),
+            remote(ref, z_send.at[k], z_recv.at[k], sides_z[step]),
         )
 
     half_order = order // 2
@@ -286,7 +288,7 @@
         for k in (0, 1):
             part = pl.ds(k * half_order, half_order)
             source = min(q, 1)
-            when = deepest + PIECES // 4 + 2 * q + k
+            when = HOP * deepest + PIECES // 4 + q
             items.append((when, source, rows.at[q // 2, 0, part], corner.at[q, part]))
     for b in (0, 1):
         for k in (0, 1):
@@ -297,20 +299,18 @@
 
     def item_copies(k, ref):
         return (
-            remote(ref, y_send.at[2 * k], y_recv.at[k], at_y(1)),
-            remote(ref, y_send.at[2 * k + 1], y_recv.at[k], at_y(-1)),
+            remote(ref, y_send.at[2 * k], y_recv.at[k], sides_y[1]),
+            remote(ref, y_send.at[2 * k + 1], y_recv.at[k], sides_y[-1]),
             remote(ref, core_send.at[k], core_recv.at[k], partner),
         )
 
-    def place(source):
-        ahead = (y + CHIPS_Y - source // 2) % CHIPS_Y
-        up = ahead < far
-        down = (ahead == 0) | (ahead > far + 1) if CHIPS_Y > 2 else ahead < 0
-        return ahead, jnp.minimum(ahead, CHIPS_Y - ahead), up, down
+
+    down = (y == 0) | (y > far + 1) if CHIPS_Y > 2 else y < 0
+    placed = y, jnp.minimum(y, CHIPS_Y - y), y < far, down
 
     def step(t, carry):
         for n, h, in_x, in_z in streams:
-            p = t - in_x - in_z
+            p = t - HOP * (in_x + in_z)
 
             @pl.when((p >= 0) & (p < PIECES))
             def _():
@@ -333,7 +333,7 @@
                     along_z.start()
 
         for k, (when, source, origin, ref) in enumerate(items):
-            ahead, depth, up, down = place(source)
+            ahead, depth, up, down = placed
             above, below, across = item_copies(k, ref)
 
             @pl.when((t == when + 2 * depth) & (core == source % 2))
@@ -364,7 +364,7 @@
 
         return carry
 
-    steps = CHIPS_X + CHIPS_Z - 2 + PIECES + 2 * far + 8
+    steps = HOP * (CHIPS_X + CHIPS_Z - 2) + max(PIECES, PIECES // 4 + 2 * far + 4) + 2
     lax.fori_loop(0, steps, step, 0)
 
     def drain(p, carry):
@@ -383,7 +383,7 @@
 
     lax.fori_loop(0, PIECES, drain, 0)
     for k, (_, source, _, ref) in enumerate(items):
-        _, _, up, down = place(source)
+        _, _, up, down = placed
         above, below, across = item_copies(k, ref)
 
         @pl.when(core == source % 2)

time: 165 us -> 112 us (0.68)
  the two profiles are of different devices: /device:TPU:92 before, /device:TPU:100 now
where the time goes in v4:
time: 112 us
  Pallas kernels  112 us (100%)
    pallas_call x1, Pallas kernels, spread(): pl.pallas_call(spread_kernel, out_shape=tuple((jax.ShapeDtypeStruct(shape...  78.9 us
    pallas_call x1, Pallas kernels, factor_second(): pl.pallas_call(second_kernel, out_shape=(SQUARE, SQUARE, SQUARE), in_spec...  11.7 us
    pallas_call x1, Pallas kernels, factor_first(): pl.pallas_call(first_kernel, out_shape=(SQUARE, SQUARE), scratch_shapes=[...  10.7 us
    pallas_call x1, Pallas kernels, trailing(): pl.pallas_call(trailing_kernel, grid=(count_r,), out_shape=jax.ShapeDtype...  10.3 us

profile of v4, /device:TPU:100, one launch (start us, length us, event | category | flops | bytes accessed | tf_op | source)
XLA Modules:
  0.0 111.6 jit_solution(10787950870014365935)
XLA Ops:
  0.0 78.9 %spread.1 = (f32[2,4,256,256]{3,2,1,0:T(8,128)}, f32[2,2,256,256]{3,2,1,0:T(8,128)}, f32[3,256,256]{2,1,0:T(8,128)}) custom-call(f32[4,2,256,256]{3,2,1,0:T(8,128)} %bitcast.4), custom_call_target="tpu_custom_call" | custom-call | tf_op jit(solution)/shard_map/spread/pallas_call | solution.py:407
  78.9 10.7 %factor_first.1 = (f32[256,256]{1,0:T(8,128)}, f32[256,256]{1,0:T(8,128)}) custom-call(f32[3,256,256]{2,1,0:T(8,128)} %get-tuple-element.15.corner_ref), custom_call_target="tpu_custom_call" | custom-call | flops 33554432 | bytes 25165824 | tf_op jit(solution)/shard_map/factor_first/pallas_call | solution.py:119
  89.7 11.7 %factor_second.1 = (f32[256,256]{1,0:T(8,128)}, f32[256,256]{1,0:T(8,128)}, f32[256,256]{1,0:T(8,128)}) custom-call(s32[2,64]{1,0:T(2,128)} %pattern.3, f32[3,256,256]{2,1,0:T(8,128)} %get-tuple-element.15.corner_ref, f32[256,256]{1,0:T(8,128)} %get-tuple-element.16.w_ref.w0_ref), custom_call_target="tpu_custom_call" | custom-call | flops 33554432 | bytes 25165824 | tf_op jit(solution)/shard_map/factor_second/pallas_call | solution.py:130
  101.3 10.3 %trailing.1 = f32[4,2,256,256]{3,2,1,0:T(8,128)} custom-call(s32[2,64]{1,0:T(2,128)} %pattern.3, f32[4,2,256,256]{3,2,1,0:T(8,128)} %bitcast.5, f32[2,4,256,256]{3,2,1,0:T(8,128)} %get-tuple-element.13.rows_ref, f32[2,2,256,256]{3,2,1,0:T(8,128)} %get-tuple-element.14.cols_ref, f32[256,256]{1,0:T(8,128)} %get-tuple-element.16.w_ref.w0_ref, ...), custom_call_target="tpu_custom_call" | custom-call | tf_op jit(solution)/shard_map/trailing/pallas_call | solution.py:204

commit v5 on v4

--- a/solution.py
+++ b/solution.py
@@ -218,8 +218,9 @@
 
 
 CHIPS_X, CHIPS_Y, CHIPS_Z = 4, 8, 8
-PIECES = 16
-HOP = 2
+PIECES = 32
+HOP = 3
+HOP_Y = 4
 MESH = pl.DeviceIdType.MESH
 
 
@@ -294,7 +295,7 @@
         for k in (0, 1):
             part = pl.ds(k * half_order, half_order)
             for n in (0, 1):
-                items.append((2 * (2 * b + k), n, blocks.at[0, b, part], cols.at[n, b, part]))
+                items.append((HOP_Y * (2 * b + k), n, blocks.at[0, b, part], cols.at[n, b, part]))
     far = CHIPS_Y // 2
 
     def item_copies(k, ref):
@@ -336,7 +337,7 @@
             ahead, depth, up, down = placed
             above, below, across = item_copies(k, ref)
 
-            @pl.when((t == when + 2 * depth) & (core == source % 2))
+            @pl.when((t == when + HOP_Y * depth) & (core == source % 2))
             def _():
                 @pl.when(ahead == 0)
                 def _():
@@ -358,13 +359,13 @@
 
                 across.start()
 
-            @pl.when((t == when + 2 * depth + 2) & (core != source % 2))
+            @pl.when((t == when + HOP_Y * (depth + 1)) & (core != source % 2))
             def _():
                 across.wait_recv()
 
         return carry
 
-    steps = HOP * (CHIPS_X + CHIPS_Z - 2) + max(PIECES, PIECES // 4 + 2 * far + 4) + 2
+    steps = HOP * (CHIPS_X + CHIPS_Z - 2) + max(PIECES, PIECES // 4 + 2 + HOP_Y * (far + 1)) + 2
     lax.fori_loop(0, steps, step, 0)
 
     def drain(p, carry):

time: 112 us -> 114 us (1.018)
  the two profiles are of different devices: /device:TPU:100 before, /device:TPU:98 now
where the time goes in v5:
time: 114 us
  Pallas kernels  114 us (100%)
    pallas_call x1, Pallas kernels, spread(): pl.pallas_call(spread_kernel, out_shape=tuple((jax.ShapeDtypeStruct(shape...  81.4 us
    pallas_call x1, Pallas kernels, factor_second(): pl.pallas_call(second_kernel, out_shape=(SQUARE, SQUARE, SQUARE), in_spec...  11.7 us
    pallas_call x1, Pallas kernels, factor_first(): pl.pallas_call(first_kernel, out_shape=(SQUARE, SQUARE), scratch_shapes=[...  10.7 us
    pallas_call x1, Pallas kernels, trailing(): pl.pallas_call(trailing_kernel, grid=(count_r,), out_shape=jax.ShapeDtype...  10.3 us

profile of v5, /device:TPU:98, one launch (start us, length us, event | category | flops | bytes accessed | tf_op | source)
XLA Modules:
  0.0 114.1 jit_solution(15242771885957448398)
XLA Ops:
  0.0 81.4 %spread.1 = (f32[2,4,256,256]{3,2,1,0:T(8,128)}, f32[2,2,256,256]{3,2,1,0:T(8,128)}, f32[3,256,256]{2,1,0:T(8,128)}) custom-call(f32[4,2,256,256]{3,2,1,0:T(8,128)} %bitcast.4), custom_call_target="tpu_custom_call" | custom-call | tf_op jit(solution)/shard_map/spread/pallas_call | solution.py:408
  81.5 10.7 %factor_first.1 = (f32[256,256]{1,0:T(8,128)}, f32[256,256]{1,0:T(8,128)}) custom-call(f32[3,256,256]{2,1,0:T(8,128)} %get-tuple-element.15.corner_ref), custom_call_target="tpu_custom_call" | custom-call | flops 33554432 | bytes 25165824 | tf_op jit(solution)/shard_map/factor_first/pallas_call | solution.py:119
  92.2 11.7 %factor_second.1 = (f32[256,256]{1,0:T(8,128)}, f32[256,256]{1,0:T(8,128)}, f32[256,256]{1,0:T(8,128)}) custom-call(s32[2,64]{1,0:T(2,128)} %pattern.3, f32[3,256,256]{2,1,0:T(8,128)} %get-tuple-element.15.corner_ref, f32[256,256]{1,0:T(8,128)} %get-tuple-element.16.w_ref.w0_ref), custom_call_target="tpu_custom_call" | custom-call | flops 33554432 | bytes 25165824 | tf_op jit(solution)/shard_map/factor_second/pallas_call | solution.py:130
  103.8 10.3 %trailing.1 = f32[4,2,256,256]{3,2,1,0:T(8,128)} custom-call(s32[2,64]{1,0:T(2,128)} %pattern.3, f32[4,2,256,256]{3,2,1,0:T(8,128)} %bitcast.5, f32[2,4,256,256]{3,2,1,0:T(8,128)} %get-tuple-element.13.rows_ref, f32[2,2,256,256]{3,2,1,0:T(8,128)} %get-tuple-element.14.cols_ref, f32[256,256]{1,0:T(8,128)} %get-tuple-element.16.w_ref.w0_ref, ...), custom_call_target="tpu_custom_call" | custom-call | tf_op jit(solution)/shard_map/trailing/pallas_call | solution.py:204
